TPU v7x, 32 devices: a whole 2x2x4 slice. The times are simulated.
32 devices in a mesh: row: 4 (over z), col: 8 (over y, x, core).
Axes of the slice: x: 2, y: 2, z: 4, core: 2. Of those that a mesh axis runs over, the one named last changes fastest.
Arguments:
- points: bfloat16 [2, 8192], P(None, ('row', 'col')), may hold values from 0 to 1
- noise_var: float32 [8192], P(('row', 'col')), may hold values from 0.5 to 2
- district: int32 [8192], P(('row', 'col')), may hold values from 0 to 63, never falling along the last dimension, each value on 1 to 512 neighbouring positions
- solution: float32 [32, 8192], P(None, ('row', 'col')), may hold values from -6 to 6
- residual: float32 [32, 8192], P(None, ('row', 'col')), may hold values from -44 to 44
- direction: float32 [32, 8192], P(None, ('row', 'col')), may hold values from -44 to 44
Outputs:
- new_solution: float32 [32, 8192], P(None, ('row', 'col'))
- new_residual: float32 [32, 8192], P(None, ('row', 'col'))
- new_direction: float32 [32, 8192], P(None, ('row', 'col'))
Inputs may be any that keep to these rules, and one draw needn't show every extreme that they name: Samples are ordered by district; every district holds 1 to 512 samples and one holds exactly 512.
All inputs are finite; a program needn't handle non-finite values.
Results may differ from a plain program's by a relative error of at most 0.004.
Values may be sent and summed in bfloat16 or wider, within the bound.
No kernel may reach another device: no remote copies, remote signals or barrier semaphores. Data moves between devices by JAX's collectives and lax.ppermute only.
A program may use at most 64 MiB of HBM per device.

v0:
```python
import math
import jax
import jax.numpy as jnp
from jax import lax
from jax.sharding import PartitionSpec as P

NDIST = 64
root_three = math.sqrt(3.0)
corr_range = 0.05
district_gain = 0.5


def matern_tile(left_points, right_points):
    left_vals = left_points.astype(jnp.float32)
    right_vals = right_points.astype(jnp.float32)
    delta_x = left_vals[0][:, None] - right_vals[0][None, :]
    delta_y = left_vals[1][:, None] - right_vals[1][None, :]
    scaled = root_three / corr_range * jnp.sqrt(delta_x * delta_x + delta_y * delta_y)
    return ((1.0 + scaled) * jnp.exp(-scaled)).astype(jnp.bfloat16)


def small_product(left, right):
    return jnp.dot(left, right, precision=lax.Precision.HIGHEST, preferred_element_type=jnp.float32)


def chol_solve(matrix, rhs_mat):
    factor = jnp.linalg.cholesky(matrix)
    return jax.scipy.linalg.cho_solve((factor, True), rhs_mat)


def per_device(points, noise_var, district, solution, residual, direction):
    local_count = points.shape[1]
    rhs_count = direction.shape[0]
    whole_count = local_count * lax.axis_size("row") * lax.axis_size("col")
    kernel_scale = 1.0 / (corr_range * math.sqrt(whole_count))
    labels = jnp.arange(NDIST, dtype=jnp.int32)
    onehot = (district[None, :] == labels[:, None]).astype(jnp.float32)
    local_sums = small_product(direction, onehot.T)
    local_sizes = jnp.sum(onehot, axis=1)
    local_norm = small_product(residual, residual.T)
    district_sums, sizes = lax.psum((local_sums, local_sizes), ("row", "col"))
    old_norm = lax.psum(local_norm, ("row", "col"))
    lowered = direction.astype(jnp.bfloat16)
    empty = jnp.zeros((rhs_count, local_count), jnp.float32)
    left_points = lax.all_gather(points, ("row", "col"), axis=1, tiled=True)
    left_dir = lax.all_gather(lowered, ("row", "col"), axis=1, tiled=True)
    width_now = left_points.shape[1]
    block_len = 8192

    def one_step(index_now, acc):
        part_points = lax.dynamic_slice_in_dim(left_points, index_now * block_len, block_len, 1)
        part_dir = lax.dynamic_slice_in_dim(left_dir, index_now * block_len, block_len, 1)
        return acc + jnp.dot(
            part_dir, matern_tile(part_points, points), preferred_element_type=jnp.float32
        )

    kernel_part = lax.fori_loop(0, width_now // block_len, one_step, empty)
    weights = district_sums / jnp.sqrt(sizes)[None, :]
    district_part = small_product(weights, onehot)
    image = (
        noise_var[None, :] * direction + kernel_part * kernel_scale + district_gain * district_part
    )
    local_curv = small_product(direction, image.T)
    curvature = lax.psum(local_curv, ("row", "col"))
    alpha = chol_solve(curvature, old_norm)
    new_solution = solution + small_product(alpha.T, direction)
    new_residual = residual - small_product(alpha.T, image)
    new_norm = lax.psum(small_product(new_residual, new_residual.T), ("row", "col"))
    beta = chol_solve(old_norm, new_norm)
    new_direction = new_residual + small_product(beta.T, direction)
    return (new_solution, new_residual, new_direction)


def solution(mesh):
    in_specs = (
        P(None, ("row", "col")),
        P(("row", "col")),
        P(("row", "col")),
        P(None, ("row", "col")),
        P(None, ("row", "col")),
        P(None, ("row", "col")),
    )
    out_specs = (P(None, ("row", "col")), P(None, ("row", "col")), P(None, ("row", "col")))
    return jax.shard_map(
        per_device, mesh=mesh, in_specs=in_specs, out_specs=out_specs, check_vma=False
    )
```

profile of v0, /device:TPU:14, one launch (start us, length us, event | category | flops | bytes accessed | tf_op | source)
XLA Modules:
  0.0 224.8 jit_solution(12056123770513564116)
XLA Ops:
  0.7 29.1 %all_gather.6 = bf16[2,8192]{1,0:T(2,128)(2,1)S(1)} all-gather(bf16[2,256]{1,0:T(2,128)(2,1)} %param.9), channel_id=1, replica_groups=mesh['row'=4,'col'=8] {'row','col'}, dimensions={1}, use_global_device_ids=true | all-gather | bytes 33792 | tf_op jit(solution)/shard_map/all_gather | solution.py:45
  29.8 0.8 fusion.24
  30.5 0.8 convert_element_type.21
  31.3 41.2 %all_gather.7 = bf16[32,8192]{1,0:T(8,128)(2,1)S(1)} all-gather(bf16[32,256]{1,0:T(8,128)(2,1)S(1)} %convert_element_type.21), channel_id=1, replica_groups=mesh['row'=4,'col'=8] {'row','col'}, dimensions={1}, use_global_device_ids=true | all-gather | bytes 540672 | tf_op jit(solution)/shard_map/all_gather | solution.py:46
  72.5 5.2 %fusion.4 = f32[32,256]{1,0:T(8,128)S(1)} fusion(bf16[32,8192]{1,0:T(8,128)(2,1)S(1)} %all_gather.7, f32[256]{0:T(256)S(1)} %bitcast.55, f32[8192]{0:T(1024)S(1)} %bitcast.53, f32[256]{0:T(256)S(1)} %bitcast.54, f32[8192]{0:T(1024)S(1)} %bitcast.52, f32[32,256]{1,0:T(8,128)S(1)} %copy-done, f32[256]{0:T(256)S(1)} %copy-done.5), kind=kOutput, calls=%fused_computation.10 | convolution fusion | flops 155213824 | bytes 658432 | tf_op jit(solution)/shard_map/while/body/eval_jaxpr/dot_general | solution.py:53
  77.7 0.2 convolution_bitcast_fusion
  78.0 49.4 %all-reduce.1 = (f32[32,64]{0,1:T(8,128)S(1)}, f32[64]{0:T(128)S(1)}) all-reduce(f32[32,64]{0,1:T(8,128)S(1)} %convolution_bitcast_fusion, f32[64]{0:T(128)S(1)} %convert_reduce_fusion), channel_id=1, replica_groups=mesh['row'=4,'col'=8] {'row','col'}, use_global_device_ids=true, to_apply=%region_0.0 | all-reduce | flops 2112 | bytes 16896 | tf_op jit(solution)/shard_map/psum | solution.py:41
  127.3 0.3 fusion.1
  127.8 0.2 fusion.25
  128.0 38.5 %all-reduce = (f32[32,32]{0,1:T(8,128)S(1)}, f32[32,32]{0,1:T(8,128)S(1)}) all-reduce(f32[32,32]{0,1:T(8,128)S(1)} %fusion.25, f32[32,32]{0,1:T(8,128)S(1)} %convolution_bitcast_fusion.1), channel_id=1, replica_groups=mesh['row'=4,'col'=8] {'row','col'}, use_global_device_ids=true, to_apply=%region_6.8 | all-reduce | flops 2048 | bytes 16384 | tf_op jit(solution)/shard_map/psum | solution.py:42
  166.6 2.9 %cholesky.55 = f32[32,32]{1,0:T(8,128)S(1)} custom-call(f32[32,32]{1,0:T(8,128)S(1)} %get-tuple-element.31), custom_call_target="Cholesky" | custom-call | tf_op jit(solution)/shard_map/jit(cholesky)/cholesky | solution.py:27
  169.6 0.6 compare_reduce_fusion
  170.2 0.7 fusion.9
  170.9 2.4 %custom-call.9 = f32[1,32,32]{1,2,0:T(8,128)S(1)} custom-call(f32[1,32,32]{2,1,0:T(8,128)S(1)} %fusion.9), custom_call_target="InvertDiagBlocksLowerTriangular" | custom-call | tf_op jit(solution)/shard_map/jit(_cho_solve)/triangular_solve | solution.py:28
  173.3 2.9 %cholesky.44 = f32[32,32]{1,0:T(8,128)S(1)} custom-call(f32[32,32]{1,0:T(8,128)S(1)} %get-tuple-element.32), custom_call_target="Cholesky" | custom-call | tf_op jit(solution)/shard_map/jit(cholesky)/cholesky | solution.py:27
  176.3 0.6 compare_reduce_fusion.1
  176.9 0.7 fusion.8
  177.6 2.4 %custom-call.8 = f32[1,32,32]{1,2,0:T(8,128)S(1)} custom-call(f32[1,32,32]{2,1,0:T(8,128)S(1)} %fusion.8), custom_call_target="InvertDiagBlocksLowerTriangular" | custom-call | tf_op jit(solution)/shard_map/jit(_cho_solve)/triangular_solve | solution.py:28
  180.0 0.2 fusion.17
  180.4 0.2 convolution_subtract_fusion
  180.8 41.9 %psum.39 = f32[32,32]{1,0:T(8,128)S(1)} all-reduce(f32[32,32]{1,0:T(8,128)S(1)} %fusion.26), channel_id=1, replica_groups=mesh['row'=4,'col'=8] {'row','col'}, use_global_device_ids=true, to_apply=%region_7.0 | all-reduce | flops 1024 | bytes 8192 | tf_op jit(solution)/shard_map/psum | solution.py:68
  222.7 0.2 fusion.12
  223.1 0.9 convolution_add_fusion
  223.9 0.8 convolution_add_fusion.1
  (24 shorter events, 1.0 us)
Async XLA Ops:
  0.6 71.8 %copy-start = (f32[32,256]{1,0:T(8,128)S(1)}, f32[32,256]{1,0:T(8,128)}, u32[]{:S(2)}) copy-start(f32[32,256]{1,0:T(8,128)} %param.14) | copy-start | bytes 98308
  0.6 71.8 %copy-start.5 = (f32[256]{0:T(256)S(1)}, f32[256]{0:T(256)}, u32[]{:S(2)}) copy-start(f32[256]{0:T(256)} %param.10) | copy-start | bytes 3076
  72.5 5.2 %copy-start.4 = (s32[256]{0:T(256)S(1)}, s32[256]{0:T(256)}, u32[]{:S(2)}) copy-start(s32[256]{0:T(256)} %param.11) | copy-start | bytes 3076
  72.5 55.3 %copy-start.2 = (f32[32,256]{1,0:T(8,128)S(1)}, f32[32,256]{1,0:T(8,128)}, u32[]{:S(2)}) copy-start(f32[32,256]{1,0:T(8,128)} %param.13) | copy-start | bytes 98308
  127.6 96.3 %copy-start.3 = (f32[32,256]{1,0:T(8,128)S(1)}, f32[32,256]{1,0:T(8,128)}, u32[]{:S(2)}) copy-start(f32[32,256]{1,0:T(8,128)} %param.12) | copy-start | bytes 98308
  180.7 44.1 %copy-start.1 = (f32[32,256]{1,0:T(8,128)}, f32[32,256]{1,0:T(8,128)S(1)}, u32[]{:S(2)}) copy-start(f32[32,256]{1,0:T(8,128)S(1)} %convolution_subtract_fusion) | copy-start | bytes 98308
where the time goes:
time: 225 us
  blocking collectives  200 us (89%)
  other arithmetic  14.3 us (6%)
  matrix products  8.78 us (4%)
    psum x1, blocking collectives, per_device(): district_sums, sizes = lax.psum((local_sums, local_sizes), ('row', 'col'))  49.4 us
    psum x1, blocking collectives, per_device(): lax.psum(small_product(new_residual, new_residual.T), ('row', 'col'))  41.9 us
    all_gather x1, blocking collectives, per_device(): left_dir = lax.all_gather(lowered, ('row', 'col'), axis=1, tiled=True)  41.2 us
    psum x1, blocking collectives, per_device(): old_norm = lax.psum(local_norm, ('row', 'col'))  38.5 us
    all_gather x1, blocking collectives, per_device(): left_points = lax.all_gather(points, ('row', 'col'), axis=1, tiled=True)  29.1 us
    another operation x6, other arithmetic, chol_solve(): factor = jnp.linalg.cholesky(matrix)  7.2 us
    another operation x4, other arithmetic, chol_solve(): return jax.scipy.linalg.cho_solve((factor, True), rhs_mat)  6.17 us
    dot_general x1, matrix products, one_step(): jnp.dot(part_dir, matern_tile(part_points, points), preferred_element_typ...  5.2 us

commit v1 on v0

--- a/solution.py
+++ b/solution.py
@@ -42,7 +42,22 @@
     old_norm = lax.psum(local_norm, ("row", "col"))
     lowered = direction.astype(jnp.bfloat16)
     empty = jnp.zeros((rhs_count, local_count), jnp.float32)
-    left_points = lax.all_gather(points, ("row", "col"), axis=1, tiled=True)
+    ways, here, turn = (
+        lax.axis_size(("row", "col")),
+        lax.axis_index(("row", "col")),
+        points.shape[1],
+    )
+    line, have = (points, 1)
+    while have < ways:
+        line = jnp.concatenate(
+            [
+                line,
+                lax.ppermute(line, ("row", "col"), [(d, (d - have) % ways) for d in range(ways)]),
+            ],
+            axis=1,
+        )
+        have = 2 * have
+    left_points = jnp.roll(line, here * turn, axis=1)
     left_dir = lax.all_gather(lowered, ("row", "col"), axis=1, tiled=True)
     width_now = left_points.shape[1]
     block_len = 8192

time: 225 us -> 209 us (0.929); the launches traced: 225 us -> 205 us
  blocking collectives: 200 us -> 152 us
  starting transfers between devices: 0 us -> 20.3 us
  waiting for transfers between devices: 0 us -> 7.48 us
    all_gather x1 -> x0, blocking collectives: 29.1 us -> none  [per_device(): left_points = lax.all_gather(points, ('row', 'col'), axis=1, tiled=True)]
    ppermute x0 -> x5, starting transfers between devices: none -> 20.3 us  [per_device(): lax.ppermute(line, ('row', 'col'), [(d, (d - have) % ways) for d in range...]
    psum x1, blocking collectives: 49.4 us -> 38.3 us  [per_device(): district_sums, sizes = lax.psum((local_sums, local_sizes), ('row', 'col'))]
    all_gather x1, blocking collectives: 41.2 us -> 33.2 us  [per_device(): left_dir = lax.all_gather(lowered, ('row', 'col'), axis=1, tiled=True)]
    ppermute x0 -> x5, waiting for transfers between devices: none -> 7.48 us  [per_device(): lax.ppermute(line, ('row', 'col'), [(d, (d - have) % ways) for d in range...]
    psum x1, blocking collectives: 38.5 us -> 42.3 us  [per_device(): old_norm = lax.psum(local_norm, ('row', 'col'))]
    psum x1, blocking collectives: 41.9 us -> 38.2 us  [per_device(): lax.psum(small_product(new_residual, new_residual.T), ('row', 'col'))]
  transfers between devices with their start and end apart: 0 -> 5, of which waited for: 0 -> 3; matrix products, arithmetic and copies ran while one was open for 0% -> 1% of each run, Pallas kernels for 0% -> 0%
where the time goes in v1:
time: 209 us; the launch traced here: 205 us
  blocking collectives  152 us (73%)
  starting transfers between devices  20.3 us (10%)
  other arithmetic  14.3 us (7%)
  matrix products  8.77 us (4%)
  waiting for transfers between devices  7.48 us (4%)
    psum x1, blocking collectives, per_device(): old_norm = lax.psum(local_norm, ('row', 'col'))  42.3 us
    psum x1, blocking collectives, per_device(): district_sums, sizes = lax.psum((local_sums, local_sizes), ('row', 'col'))  38.3 us
    psum x1, blocking collectives, per_device(): lax.psum(small_product(new_residual, new_residual.T), ('row', 'col'))  38.2 us
    all_gather x1, blocking collectives, per_device(): left_dir = lax.all_gather(lowered, ('row', 'col'), axis=1, tiled=True)  33.2 us
    ppermute x5, starting transfers between devices, per_device(): lax.ppermute(line, ('row', 'col'), [(d, (d - have) % ways) for d in range...  20.3 us
    ppermute x5, waiting for transfers between devices, per_device(): lax.ppermute(line, ('row', 'col'), [(d, (d - have) % ways) for d in range...  7.48 us
    another operation x6, other arithmetic, chol_solve(): factor = jnp.linalg.cholesky(matrix)  7.2 us
    another operation x4, other arithmetic, chol_solve(): return jax.scipy.linalg.cho_solve((factor, True), rhs_mat)  6.17 us
  transfers between devices with their start and end apart: 5, of which 3 were waited for; matrix products, arithmetic and copies ran while one was open for 1% of the time, Pallas kernels for 0%

profile of v1, /device:TPU:14, one launch (start us, length us, event | category | flops | bytes accessed | tf_op | source)
XLA Modules:
  0.0 205.0 jit_solution(15118393742832450573)
XLA Ops:
  0.7 0.7 fusion.24
  1.5 0.8 convert_element_type.21
  2.2 33.2 %all_gather.3 = bf16[32,8192]{1,0:T(8,128)(2,1)S(1)} all-gather(bf16[32,256]{1,0:T(8,128)(2,1)S(1)} %convert_element_type.21), channel_id=1, replica_groups=mesh['row'=4,'col'=8] {'row','col'}, dimensions={1}, use_global_device_ids=true | all-gather | bytes 540672 | tf_op jit(solution)/shard_map/all_gather | solution.py:61
  35.9 0.6 collective-permute-start.1
  36.5 4.8 %collective-permute-done.1 = bf16[2,512]{1,0:T(2,128)(2,1)S(1)} collective-permute-done((bf16[2,512]{1,0:T(2,128)(2,1)S(1)}, bf16[2,512]{1,0:T(2,128)(2,1)S(1)}, u32[]{:S(2)}, u32[]{:S(2)}) %collective-permute-start.1) | collective-permute-done | bytes 2080 | tf_op jit(solution)/shard_map/ppermute | solution.py:55
  41.3 3.3 %collective-permute-start.2 = (bf16[2,1024]{1,0:T(2,128)(2,1)S(1)}, bf16[2,1024]{1,0:T(2,128)(2,1)S(1)}, u32[]{:S(2)}, u32[]{:S(2)}) collective-permute-start(bf16[2,1024]{1,0:T(2,128)(2,1)S(1)} %pad_maximum_fusion.1), channel_id=1, source_target_pairs={{0,28},{1,29},{2,30},{3,31},{4,0},{5,1},{6,2},{7,3},{8,4},{9,5},{1... | collective-permute-start | bytes 12296 | tf_op jit(solution)/shard_map/ppermute | solution.py:55
  44.6 1.3 collective-permute-done.2
  46.0 6.9 %collective-permute-start.3 = (bf16[2,2048]{1,0:T(2,128)(2,1)S(1)}, bf16[2,2048]{1,0:T(2,128)(2,1)S(1)}, u32[]{:S(2)}, u32[]{:S(2)}) collective-permute-start(bf16[2,2048]{1,0:T(2,128)(2,1)S(1)} %pad_maximum_fusion), channel_id=1, source_target_pairs={{0,24},{1,25},{2,26},{3,27},{4,28},{5,29},{6,30},{7,31},{8,0},{9,1... | collective-permute-start | bytes 24584 | tf_op jit(solution)/shard_map/ppermute | solution.py:55
  52.9 1.4 collective-permute-done.3
  54.3 9.5 %collective-permute-start.4 = (bf16[2,4096]{1,0:T(2,128)(2,1)S(1)}, bf16[2,4096]{1,0:T(2,128)(2,1)S(1)}, u32[]{:S(2)}, u32[]{:S(2)}) collective-permute-start(bf16[2,4096]{1,0:T(2,128)(2,1)S(1)} %get-tuple-element.29), channel_id=1, source_target_pairs={{0,16},{1,17},{2,18},{3,19},{4,20},{5,21},{6,22},{7,23},{8,24},{9,... | collective-permute-start | bytes 49160 | tf_op jit(solution)/shard_map/ppermute | solution.py:55
  63.8 38.3 %all-reduce.1 = (f32[32,64]{0,1:T(8,128)S(1)}, f32[64]{0:T(128)S(1)}) all-reduce(f32[32,64]{0,1:T(8,128)S(1)} %convolution_bitcast_fusion, f32[64]{0:T(128)S(1)} %convert_reduce_fusion), channel_id=1, replica_groups=mesh['row'=4,'col'=8] {'row','col'}, use_global_device_ids=true, to_apply=%region_0.0 | all-reduce | flops 2112 | bytes 16896 | tf_op jit(solution)/shard_map/psum | solution.py:41
  102.4 5.2 %fusion.4 = f32[32,256]{1,0:T(8,128)S(1)} fusion(bf16[32,8192]{1,0:T(8,128)(2,1)S(1)} %all_gather.3, f32[256]{0:T(256)S(1)} %bitcast.55, f32[8192]{0:T(1024)S(1)} %bitcast.53, f32[256]{0:T(256)S(1)} %bitcast.54, f32[8192]{0:T(1024)S(1)} %bitcast.52, f32[32,256]{1,0:T(8,128)S(1)} %copy-done, f32[256]{0:T(256)S(1)} %copy-done.6), kind=kOutput, calls=%fused_computation.10 | convolution fusion | flops 155213824 | bytes 658432 | tf_op jit(solution)/shard_map/while/body/eval_jaxpr/dot_general | solution.py:68
  108.1 42.3 %all-reduce = (f32[32,32]{0,1:T(8,128)S(1)}, f32[32,32]{0,1:T(8,128)S(1)}) all-reduce(f32[32,32]{0,1:T(8,128)S(1)} %fusion.25, f32[32,32]{0,1:T(8,128)S(1)} %convolution_bitcast_fusion.1), channel_id=1, replica_groups=mesh['row'=4,'col'=8] {'row','col'}, use_global_device_ids=true, to_apply=%region_6.8 | all-reduce | flops 2048 | bytes 16384 | tf_op jit(solution)/shard_map/psum | solution.py:42
  150.5 2.9 %cholesky.55 = f32[32,32]{1,0:T(8,128)S(1)} custom-call(f32[32,32]{1,0:T(8,128)S(1)} %get-tuple-element.41), custom_call_target="Cholesky" | custom-call | tf_op jit(solution)/shard_map/jit(cholesky)/cholesky | solution.py:27
  153.5 0.6 compare_reduce_fusion
  154.1 0.7 fusion.9
  154.8 2.4 %custom-call.9 = f32[1,32,32]{1,2,0:T(8,128)S(1)} custom-call(f32[1,32,32]{2,1,0:T(8,128)S(1)} %fusion.9), custom_call_target="InvertDiagBlocksLowerTriangular" | custom-call | tf_op jit(solution)/shard_map/jit(_cho_solve)/triangular_solve | solution.py:28
  157.2 2.9 %cholesky.44 = f32[32,32]{1,0:T(8,128)S(1)} custom-call(f32[32,32]{1,0:T(8,128)S(1)} %get-tuple-element.42), custom_call_target="Cholesky" | custom-call | tf_op jit(solution)/shard_map/jit(cholesky)/cholesky | solution.py:27
  160.2 0.6 compare_reduce_fusion.1
  160.8 0.7 fusion.8
  161.5 2.4 %custom-call.8 = f32[1,32,32]{1,2,0:T(8,128)S(1)} custom-call(f32[1,32,32]{2,1,0:T(8,128)S(1)} %fusion.8), custom_call_target="InvertDiagBlocksLowerTriangular" | custom-call | tf_op jit(solution)/shard_map/jit(_cho_solve)/triangular_solve | solution.py:28
  164.7 38.2 %psum.39 = f32[32,32]{1,0:T(8,128)S(1)} all-reduce(f32[32,32]{1,0:T(8,128)S(1)} %fusion.26), channel_id=1, replica_groups=mesh['row'=4,'col'=8] {'row','col'}, use_global_device_ids=true, to_apply=%region_7.10 | all-reduce | flops 1024 | bytes 8192 | tf_op jit(solution)/shard_map/psum | solution.py:83
  203.3 0.9 convolution_add_fusion
  204.2 0.8 convolution_add_fusion.1
  (51 shorter events, 2.6 us)
Async XLA Ops:
  0.6 35.2 %copy-start.3 = (bf16[2,256]{1,0:T(2,128)(2,1)S(1)}, bf16[2,256]{1,0:T(2,128)(2,1)}, u32[]{:S(2)}) copy-start(bf16[2,256]{1,0:T(2,128)(2,1)} %param.9) | copy-start | bytes 3076
  0.6 34.8 %copy-start = (f32[32,256]{1,0:T(8,128)S(1)}, f32[32,256]{1,0:T(8,128)}, u32[]{:S(2)}) copy-start(f32[32,256]{1,0:T(8,128)} %param.14) | copy-start | bytes 98308
  0.7 34.8 %copy-start.5 = (s32[256]{0:T(256)S(1)}, s32[256]{0:T(256)}, u32[]{:S(2)}) copy-start(s32[256]{0:T(256)} %param.11) | copy-start | bytes 3076
  0.7 35.0 %copy-start.2 = (f32[32,256]{1,0:T(8,128)S(1)}, f32[32,256]{1,0:T(8,128)}, u32[]{:S(2)}) copy-start(f32[32,256]{1,0:T(8,128)} %param.13) | copy-start | bytes 98308
  0.7 35.2 %collective-permute-start = (bf16[2,256]{1,0:T(2,128)(2,1)}, bf16[2,256]{1,0:T(2,128)(2,1)S(1)}, u32[]{:S(2)}, u32[]{:S(2)}) collective-permute-start(bf16[2,256]{1,0:T(2,128)(2,1)} %param.9), channel_id=1, source_target_pairs={{0,31},{1,0},{2,1},{3,2},{4,3},{5,4},{6,5},{7,6},{8,7},{9,8},{10,9... | collective-permute-start | bytes 3080 | tf_op jit(solution)/shard_map/ppermute | solution.py:55
  2.2 100.2 %copy-start.6 = (f32[256]{0:T(256)S(1)}, f32[256]{0:T(256)}, u32[]{:S(2)}) copy-start(f32[256]{0:T(256)} %param.10) | copy-start | bytes 3076
  35.9 5.4 %collective-permute-start.1 = (bf16[2,512]{1,0:T(2,128)(2,1)S(1)}, bf16[2,512]{1,0:T(2,128)(2,1)S(1)}, u32[]{:S(2)}, u32[]{:S(2)}) collective-permute-start(bf16[2,512]{1,0:T(2,128)(2,1)S(1)} %pad_maximum_fusion.2), channel_id=1, source_target_pairs={{0,30},{1,31},{2,0},{3,1},{4,2},{5,3},{6,4},{7,5},{8,6},{9,7},{10,... | collective-permute-start | bytes 6152 | tf_op jit(solution)/shard_map/ppermute | solution.py:55
  41.3 4.6 %collective-permute-start.2 = (bf16[2,1024]{1,0:T(2,128)(2,1)S(1)}, bf16[2,1024]{1,0:T(2,128)(2,1)S(1)}, u32[]{:S(2)}, u32[]{:S(2)}) collective-permute-start(bf16[2,1024]{1,0:T(2,128)(2,1)S(1)} %pad_maximum_fusion.1), channel_id=1, source_target_pairs={{0,28},{1,29},{2,30},{3,31},{4,0},{5,1},{6,2},{7,3},{8,4},{9,5},{1... | collective-permute-start | bytes 12296 | tf_op jit(solution)/shard_map/ppermute | solution.py:55
  46.0 8.3 %collective-permute-start.3 = (bf16[2,2048]{1,0:T(2,128)(2,1)S(1)}, bf16[2,2048]{1,0:T(2,128)(2,1)S(1)}, u32[]{:S(2)}, u32[]{:S(2)}) collective-permute-start(bf16[2,2048]{1,0:T(2,128)(2,1)S(1)} %pad_maximum_fusion), channel_id=1, source_target_pairs={{0,24},{1,25},{2,26},{3,27},{4,28},{5,29},{6,30},{7,31},{8,0},{9,1... | collective-permute-start | bytes 24584 | tf_op jit(solution)/shard_map/ppermute | solution.py:55
  54.3 47.9 %collective-permute-start.4 = (bf16[2,4096]{1,0:T(2,128)(2,1)S(1)}, bf16[2,4096]{1,0:T(2,128)(2,1)S(1)}, u32[]{:S(2)}, u32[]{:S(2)}) collective-permute-start(bf16[2,4096]{1,0:T(2,128)(2,1)S(1)} %get-tuple-element.29), channel_id=1, source_target_pairs={{0,16},{1,17},{2,18},{3,19},{4,20},{5,21},{6,22},{7,23},{8,24},{9,... | collective-permute-start | bytes 49160 | tf_op jit(solution)/shard_map/ppermute | solution.py:55
  107.6 96.5 %copy-start.4 = (f32[32,256]{1,0:T(8,128)S(1)}, f32[32,256]{1,0:T(8,128)}, u32[]{:S(2)}) copy-start(f32[32,256]{1,0:T(8,128)} %param.12) | copy-start | bytes 98308
  164.6 40.5 %copy-start.1 = (f32[32,256]{1,0:T(8,128)}, f32[32,256]{1,0:T(8,128)S(1)}, u32[]{:S(2)}) copy-start(f32[32,256]{1,0:T(8,128)S(1)} %convolution_subtract_fusion) | copy-start | bytes 98308
